TPU v7x, 32 devices: a whole 2x2x4 slice. The times are simulated.
32 devices in a mesh: lon: 8 (over z, x), lat: 4 (over y, core).
Axes of the slice: x: 2, y: 2, z: 4, core: 2. Of those that a mesh axis runs over, the one named last changes fastest.
Arguments:
- ocean_state: float32 [512, 4, 2, 1024], P('lat', None, None, 'lon'), may hold values from -4 to 4
- cotangent: float32 [512, 4, 2, 1024], P('lat', None, None, 'lon'), may hold values from -6 to 6
- features: bfloat16 [512, 64, 1024], P('lat', None, 'lon'), may hold values from -6 to 6
- w_in: bfloat16 [64, 256], replicated, may hold values from -0.75 to 0.75
- bias_in: float32 [256], replicated, may hold values from -3 to 3
- w_mid: bfloat16 [1, 256, 256], replicated, may hold values from -0.375 to 0.375
- w_out: bfloat16 [256, 2], replicated, may hold values from -0.375 to 0.375
- bias_out: float32 [2], replicated, may hold values from -3 to 3
- land_mask: int32 [512, 1024], P('lat', 'lon'), may hold values from 0 to 1, as said below
- home_slot: int32 [512, 8], P('lat', 'lon'), may hold values from -1 to 127, as said below
- owner_list: int32 [128, 8], P('lat', 'lon'), may hold values from 0 to 127, as said below
Outputs:
- new_state: float32 [512, 4, 2, 1024], P('lat', None, None, 'lon')
- state_adjoint: float32 [512, 4, 2, 1024], P('lat', None, None, 'lon')
- grad_w_in: float32 [64, 256], replicated
- grad_bias_in: float32 [256], replicated
- grad_w_mid: float32 [1, 256, 256], replicated
- grad_w_out: float32 [256, 2], replicated
- grad_bias_out: float32 [2], replicated
Inputs may be any that keep to these rules, and one draw needn't show every extreme that they name: `land_mask`: A block is the 128 columns of one latitude row on one index of lon. Exactly half of the blocks of each latitude band hold a sea column; blocks without sea are all land; in every band some index of lon has sea in all its blocks. `home_slot`: -1 for a block without sea; else o * 16 + c: the block is the c-th that its device sends to owner o (the device of lon index o in the same band); a device uses the slots of one owner from c = 0 up. Every owner is sent exactly 64 blocks of its band, and in every band some device fills all its slots. `owner_list`: row b * 32 + r, column o: the r-th block that owner o of band b processes, as s * 16 + c, the block of lon index s whose home_slot is o * 16 + c. The entries of one owner are distinct; every owner lists exactly 32 of the blocks sent to it, and a sea block that its owner does not list is not processed.
All inputs are finite; a program needn't handle non-finite values.
Results may differ from a plain program's by a relative error of at most 0.0063.
The roundings to bfloat16 on the way count: a program that leaves them out, or rounds other values in their place, can miss the bound.
Values may be sent and summed in bfloat16 or wider, within the bound.
A program may use at most 64 MiB of HBM per device.

v0:
```python
import math

import jax
import jax.numpy as jnp
from jax import lax
from jax.sharding import PartitionSpec as P

kappa_most = 0.2


def with_halo(block, sides, width):
    for axis, dim in sides:
        count = lax.axis_size(axis)
        forward = [(i, i + 1) for i in range(count - 1)]
        forward.append((count - 1, 0))
        backward = [(target, source) for source, target in forward]
        low = lax.ppermute(
            lax.slice_in_dim(block, block.shape[dim] - width, None, axis=dim), axis, forward
        )
        high = lax.ppermute(lax.slice_in_dim(block, 0, width, axis=dim), axis, backward)
        block = jnp.concatenate([low, block, high], axis=dim)
    return block


def local_update(state_pad, kappa_pad, sea_pad):
    east_open = (sea_pad[1:-1, :-1] * sea_pad[1:-1, 1:])[:, None, :]
    east_speed = 0.5 * (state_pad[1:-1, 2, :, :-1] + state_pad[1:-1, 2, :, 1:]) * east_open
    east_kappa = 0.5 * (kappa_pad[1:-1, :, :-1] + kappa_pad[1:-1, :, 1:]) * east_open
    west_side = state_pad[1:-1, :, :, :-1]
    east_side = state_pad[1:-1, :, :, 1:]
    east_flux = east_speed[:, None] * 0.5 * (west_side + east_side) - east_kappa[:, None] * (
        east_side - west_side
    )
    north_open = (sea_pad[:-1, 1:-1] * sea_pad[1:, 1:-1])[:, None, :]
    north_speed = 0.5 * (state_pad[:-1, 3, :, 1:-1] + state_pad[1:, 3, :, 1:-1]) * north_open
    north_kappa = 0.5 * (kappa_pad[:-1, :, 1:-1] + kappa_pad[1:, :, 1:-1]) * north_open
    south_side = state_pad[:-1, :, :, 1:-1]
    north_side = state_pad[1:, :, :, 1:-1]
    north_flux = north_speed[:, None] * 0.5 * (south_side + north_side) - north_kappa[:, None] * (
        north_side - south_side
    )
    centre = state_pad[1:-1, :, :, 1:-1]
    return centre - (east_flux[..., 1:] - east_flux[..., :-1]) - (north_flux[1:] - north_flux[:-1])


def edge_once(values):
    return with_halo(values, (("lon", 2), ("lat", 0)), 1)


def return_rims(values):
    return with_halo(values.astype(jnp.bfloat16), (("lon", 2), ("lat", 0)), 1).astype(values.dtype)


def to_owners(blocks, home_slots, owned_entries):
    owner_count = lax.axis_size("lon")
    slot_total = blocks.shape[0]
    target = jnp.where(home_slots >= 0, home_slots, slot_total)
    buffer = jnp.zeros(blocks.shape, blocks.dtype).at[target].set(blocks, mode="drop")
    buffer = buffer.reshape(
        owner_count, slot_total // owner_count, blocks.shape[1], blocks.shape[2]
    )
    arrived = lax.all_to_all(buffer, "lon", split_axis=0, concat_axis=0, tiled=True)
    arrived = arrived.reshape(slot_total, blocks.shape[1], blocks.shape[2])
    return jnp.take(arrived, owned_entries, axis=0)


def to_homes(owned, home_slots, owned_entries):
    owner_count = lax.axis_size("lon")
    slot_total = home_slots.shape[0]
    buffer = (
        jnp.zeros((slot_total, owned.shape[1], owned.shape[2]), jnp.float32)
        .at[owned_entries]
        .set(owned)
    )
    buffer = buffer.reshape(owner_count, slot_total // owner_count, owned.shape[1], owned.shape[2])
    returned = lax.all_to_all(
        buffer.astype(jnp.bfloat16), "lon", split_axis=0, concat_axis=0, tiled=True
    ).astype(buffer.dtype)
    returned = returned.reshape(slot_total, owned.shape[1], owned.shape[2])
    picked = jnp.take(returned, jnp.maximum(home_slots, 0), axis=0)
    return picked * (home_slots >= 0).astype(jnp.float32)[:, None, None]


def closure_forward(inputs, w_in, bias_in, w_mid, w_out, bias_out):
    first = (
        jnp.einsum("fh,bfc->bhc", w_in, inputs, preferred_element_type=jnp.float32)
        + bias_in[None, :, None]
    )
    hidden = jnp.tanh(first).astype(jnp.bfloat16)
    layers = [hidden]
    hidden = jnp.tanh(
        jnp.einsum("gh,bgc->bhc", w_mid[0], hidden, preferred_element_type=jnp.float32)
    ).astype(jnp.bfloat16)
    layers.append(hidden)
    logits = (
        jnp.einsum("hl,bhc->blc", w_out, hidden, preferred_element_type=jnp.float32)
        + bias_out[None, :, None]
    )
    return (layers, jax.nn.sigmoid(logits))


def closure_backward(inputs, layers, squashed, kappa_float, w_mid, w_out):
    logit_grad = kappa_float * (kappa_most * squashed * (1.0 - squashed))
    logit_low = logit_grad.astype(jnp.bfloat16)
    sum_out = jnp.einsum("bhc,blc->hl", layers[-1], logit_low, preferred_element_type=jnp.float32)
    sum_bias_out = jnp.sum(logit_grad, axis=(0, 2))
    carried = jnp.einsum("hl,blc->bhc", w_out, logit_low, preferred_element_type=jnp.float32)
    mid_sums = []
    current = layers[1].astype(jnp.float32)
    layer_grad = (carried * (1.0 - current * current)).astype(jnp.bfloat16)
    mid_sums.insert(
        0, jnp.einsum("bgc,bhc->gh", layers[0], layer_grad, preferred_element_type=jnp.float32)
    )
    carried = jnp.einsum("gh,bhc->bgc", w_mid[0], layer_grad, preferred_element_type=jnp.float32)
    base_float = layers[0].astype(jnp.float32)
    first_grad = carried * (1.0 - base_float * base_float)
    sum_bias_in = jnp.sum(first_grad, axis=(0, 2))
    sum_in = jnp.einsum(
        "bfc,bhc->fh", inputs, first_grad.astype(jnp.bfloat16), preferred_element_type=jnp.float32
    )
    return (sum_in, sum_bias_in, jnp.stack(mid_sums), sum_out, sum_bias_out)


def on_device(
    ocean_state,
    cotangent,
    features,
    w_in,
    bias_in,
    w_mid,
    w_out,
    bias_out,
    land_mask,
    home_slot,
    owner_list,
):
    row_count, field_count, level_count, col_count = ocean_state.shape
    flat_width = field_count * level_count
    home_slots = home_slot[:, 0]
    owned_entries = owner_list[:, 0]
    sea_layer = land_mask.astype(jnp.float32)[:, None, :]
    fields_flat = jnp.concatenate(
        [ocean_state.reshape(row_count, flat_width, col_count), sea_layer], axis=1
    )
    reach = 1
    field_channels = fields_flat.shape[1]
    inputs = to_owners(features, home_slots, owned_entries)
    layers, squashed = closure_forward(inputs, w_in, bias_in, w_mid, w_out, bias_out)
    diffusivity = to_homes(kappa_most * squashed, home_slots, owned_entries)
    wide_all = edge_once(jnp.concatenate([fields_flat, diffusivity], axis=1))
    wide_fields = wide_all[:, :field_channels]
    wide_kappa = wide_all[:, field_channels:]
    lat_index = lax.axis_index("lat")
    lat_count = lax.axis_size("lat")
    wide_rows = row_count + 2 * reach
    row_ids = lax.broadcasted_iota(jnp.int32, (wide_rows,), 0)
    south_inside = (row_ids >= reach) | (lat_index > 0)
    north_inside = (row_ids < row_count + reach) | (lat_index < lat_count - 1)
    row_gate = (south_inside & north_inside).astype(jnp.float32)
    sea_wide = wide_fields[:, flat_width] * row_gate[:, None]
    state_wide = wide_fields[:, :flat_width].reshape(
        wide_rows, field_count, level_count, col_count + 2 * reach
    )

    def stepper(state_in, kappa_in):
        return local_update(state_in, kappa_in, sea_wide)

    new_state, pullback = jax.vjp(stepper, state_wide, wide_kappa)
    state_grad_pad, kappa_grad_pad = pullback(cotangent)
    grads_wide = jnp.concatenate(
        [state_grad_pad.reshape(row_count + 2, flat_width, col_count + 2), kappa_grad_pad], axis=1
    )
    interior = grads_wide[1:-1, :, 1:-1]
    channels = interior.shape[1]
    lon_rims = (
        jnp.zeros_like(interior)
        .at[:, :, 0]
        .set(grads_wide[1:-1, :, 0])
        .at[:, :, -1]
        .set(grads_wide[1:-1, :, -1])
    )
    lat_rims = (
        jnp.zeros_like(interior)
        .at[0]
        .set(grads_wide[0, :, 1:-1])
        .at[-1]
        .set(grads_wide[-1, :, 1:-1])
    )
    returned = return_rims(jnp.concatenate([lon_rims, lat_rims], axis=1))
    summed = interior.at[:, :, 0].add(returned[1:-1, :channels, 0])
    summed = summed.at[:, :, -1].add(returned[1:-1, :channels, -1])
    summed = summed.at[0].add(returned[0, channels:, 1:-1])
    summed = summed.at[-1].add(returned[-1, channels:, 1:-1])
    state_adjoint = summed[:, :flat_width].reshape(ocean_state.shape)
    kappa_low = summed[:, flat_width:].astype(jnp.bfloat16)
    kappa_owned = to_owners(kappa_low, home_slots, owned_entries).astype(jnp.float32)
    local_terms = closure_backward(inputs, layers, squashed, kappa_owned, w_mid, w_out)
    totals = lax.psum(
        (local_terms[0], local_terms[1], local_terms[2], local_terms[3], local_terms[4]),
        ("lon", "lat"),
    )
    scaling = 1.0 / math.sqrt(row_count * col_count)
    return (
        new_state,
        state_adjoint,
        totals[0] * scaling,
        totals[1] * scaling,
        totals[2] * scaling,
        totals[3] * scaling,
        totals[4] * scaling,
    )


def solution(mesh):
    in_specs = (
        P("lat", None, None, "lon"),
        P("lat", None, None, "lon"),
        P("lat", None, "lon"),
        P(),
        P(),
        P(),
        P(),
        P(),
        P("lat", "lon"),
        P("lat", "lon"),
        P("lat", "lon"),
    )
    out_specs = (P("lat", None, None, "lon"), P("lat", None, None, "lon"), P(), P(), P(), P(), P())
    return jax.shard_map(
        on_device, mesh=mesh, in_specs=in_specs, out_specs=out_specs, check_vma=False
    )
```

profile of v0, /device:TPU:1, one launch (start us, length us, event | category | flops | bytes accessed | tf_op | source)
XLA Modules:
  0.0 460.8 jit_solution(15768047106622952651)
XLA Ops:
  8.0 1.8 broadcast_in_dim.66
  9.8 15.7 %scatter_fusion = bf16[128,64,128]{2,1,0:T(8,128)(2,1)} fusion(bf16[128,64,128]{2,1,0:T(8,128)(2,1)} %broadcast_in_dim.66, s32[128]{0:T(128)S(1)} %get-tuple-element.188, bf16[128,64,128]{2,1,0:T(8,128)(2,1)S(1)} %copy-done.25), kind=kCustom, calls=%fused_computation.3 | custom fusion | bytes 6291968 | tf_op jit(solution)/shard_map/scatter | solution.py:58
  25.6 5.5 %all-to-all-start = ((bf16[8,16,64,128]{3,2,1,0:T(8,128)(2,1)}), bf16[8,16,64,128]{3,2,1,0:T(8,128)(2,1)S(1)}, u32[]{:S(2)}, u32[]{:S(2)}) async-start(bf16[8,16,64,128]{3,2,1,0:T(8,128)(2,1)} %bitcast.6), calls=%async_computation | async-start | bytes 4194304 | tf_op jit(solution)/shard_map/all_to_all | solution.py:62
  31.3 46.1 %all-to-all-done = bf16[8,16,64,128]{3,2,1,0:T(8,128)(2,1)S(1)} async-done(((bf16[8,16,64,128]{3,2,1,0:T(8,128)(2,1)}), bf16[8,16,64,128]{3,2,1,0:T(8,128)(2,1)S(1)}, u32[]{:S(2)}, u32[]{:S(2)}) %all-to-all-start) | async-done | bytes 2097184 | tf_op jit(solution)/shard_map/all_to_all | solution.py:62
  84.3 5.7 %all-to-all-start.1 = ((bf16[8,16,2,128]{3,2,1,0:T(2,128)(2,1)}), bf16[8,16,2,128]{3,2,1,0:T(2,128)(2,1)S(1)}, u32[]{:S(2)}, u32[]{:S(2)}) async-start(bf16[8,16,2,128]{3,2,1,0:T(2,128)(2,1)} %bitcast.15), calls=%async_computation.1 | async-start | bytes 131072 | tf_op jit(solution)/shard_map/all_to_all | solution.py:76
  90.4 5.5 %all-to-all-done.1 = bf16[8,16,2,128]{3,2,1,0:T(2,128)(2,1)S(1)} async-done(((bf16[8,16,2,128]{3,2,1,0:T(2,128)(2,1)}), bf16[8,16,2,128]{3,2,1,0:T(2,128)(2,1)S(1)}, u32[]{:S(2)}, u32[]{:S(2)}) %all-to-all-start.1) | async-done | bytes 65568 | tf_op jit(solution)/shard_map/all_to_all | solution.py:76
  99.5 3.4 collective-permute-done
  105.9 3.1 collective-permute-start.3
  109.0 2.2 copy.222
  114.4 1.9 copy.224
  116.3 1.9 pad_maximum_fusion
  119.3 1.8 fusion.63
  126.7 1.9 fusion.26
  128.6 1.7 copy.240
  130.3 1.7 copy.269
  132.1 1.7 copy.270
  133.8 2.2 copy.272
  136.0 2.2 copy.271
  138.2 2.3 copy.268
  140.5 2.3 copy.267
  144.9 1.8 copy.232
  147.7 1.7 copy.266
  150.8 5.6 %multiply_reduce_fusion = (f32[128,2,129]{2,1,0:T(2,128)S(1)}, f32[128,2,129]{2,1,0:T(2,128)S(1)}, f32[128,4,2,129]{3,2,1,0:T(2,128)}, f32[128,4,2,129]{3,2,1,0:T(2,128)S(1)}, f32[128,4,2,129]{3,2,1,0:T(2,128)S(1)}) fusion(f32[128,4,2,129]{3,2,1,0:T(2,128)} %copy.268, f32[128,4,2,129]{3,2,1,0:T(2,128)} %copy.267, f32[128,4,2,128]{3,2,1,0:T(2,128)S(1)} %copy-done.17, ...), kind=kLoop, calls=%fused_computation.41 | loop fusion | flops 2047488 | bytes 4218880 | tf_op jit(solution)/shard_map/transpose(jvp())/reduce_sum | solution.py:31
  157.6 3.0 multiply_reduce_fusion.2
  160.7 7.5 %pad_add_fusion = f32[130,4,2,130]{3,2,1,0:T(2,128)} fusion(f32[128,1,2,129]{3,2,1,0:T(2,128)S(1)} %fusion.27, f32[128,4,2,129]{3,2,1,0:T(2,128)S(1)} %get-tuple-element.162, f32[128,4,2,129]{3,2,1,0:T(2,128)S(1)} %get-tuple-element.161, f32[129,1,2,128]{3,2,1,0:T(2,128)S(1)} %fusion.31, f32[129,4,2,128]{3,2,1,0:T(2,128)S(1)} %get-tuple-element.178, ...), kind=kLoop, calls=%fused_computation.35 | loop fusion | flops 1081600 | bytes 3442816 | tf_op jit(solution)/shard_map/transpose(jvp())/add_any | solution.py:27
  168.1 3.0 reshape.406
  171.2 2.0 copy.263
  180.1 1.9 copy.244
  182.0 2.1 pad_maximum_fusion.1
  186.6 12.2 %scatter.46 = bf16[128,10,128]{0,1,2:T(8,128)(2,1)} dynamic-update-slice(bf16[128,10,128]{0,1,2:T(8,128)(2,1)} %scatter.45, bf16[1,10,128]{0,1,2:T(8,128)(2,1)} %get-tuple-element.163, s32[]{:T(128)} %constant.251.clone.1, s32[]{:T(128)} %constant.250.clone.1, s32[]{:T(128)} %constant.250.clone.1) | dynamic-update-slice | bytes 5124 | tf_op jit(solution)/shard_map/scatter | solution.py:187
  202.1 2.8 collective-permute-done.4
  207.8 1.7 copy.246
  211.0 1.7 copy.245
  213.9 2.3 fusion.22
  216.2 2.2 slice.363
  218.5 2.0 copy.264
  226.5 2.4 convert_add_fusion
  229.0 4.2 scatter-add.16
  233.1 2.6 slice_add_fusion
  235.8 12.0 %scatter-add.19 = f32[128,10,128]{0,1,2:T(8,128)} dynamic-update-slice(f32[128,10,128]{0,1,2:T(8,128)} %scatter-add.16, f32[1,10,128]{0,1,2:T(8,128)} %slice_add_fusion, s32[]{:T(128)} %constant.251.clone.1, s32[]{:T(128)} %constant.250.clone.1, s32[]{:T(128)} %constant.250.clone.1) | dynamic-update-slice | bytes 10244 | tf_op jit(solution)/shard_map/scatter-add | solution.py:193
  249.7 14.3 %scatter_fusion.2 = bf16[128,2,128]{2,1,0:T(2,128)(2,1)} fusion(bf16[128,2,128]{2,1,0:T(2,128)(2,1)} %broadcast_in_dim.70, s32[128]{0:T(128)S(1)} %copy-done.46, bf16[128,2,128]{2,1,0:T(2,128)(2,1)S(1)} %copy.249), kind=kCustom, calls=%fused_computation.5 | custom fusion | bytes 197120 | tf_op jit(solution)/shard_map/scatter | solution.py:58
  264.0 3.4 all-to-all-start.2
  267.5 3.3 fusion.23
  271.7 1.9 copy.257
  274.5 2.5 fusion
  282.3 40.0 %all-reduce.19 = (f32[256]{0:T(256)S(1)}, f32[256,2]{0,1:T(2,128)S(1)}, f32[2]{0:T(128)S(1)}) all-reduce(f32[256]{0:T(256)S(1)} %get-tuple-element.189, f32[256,2]{0,1:T(2,128)S(1)} %fusion.18, f32[2]{0:T(128)S(1)} %get-tuple-element.183), channel_id=1, replica_groups=mesh['lon'=8,'lat'=4] {'lon','lat'}, use_global_device_ids=true, to_apply=%region_9.10 | all-reduce | flops 770 | bytes 6160 | tf_op jit(solution)/shard_map/psum | solution.py:198
  324.0 126.8 %all-reduce.23.cloned.1.call-done = (f32[64,256]{1,0:T(8,128)}, f32[1,256,256]{2,1,0:T(8,128)}) async-done(((f32[64,256]{1,0:T(8,128)}, f32[1,256,256]{2,1,0:T(8,128)}), (f32[64,256]{1,0:T(8,128)}, f32[1,256,256]{2,1,0:T(8,128)})) %all-reduce.23.cloned.1.call-update) | async-done | bytes 327696 | tf_op jit(solution)/shard_map/psum | solution.py:198
  452.3 1.7 broadcast_multiply_fusion
  (195 shorter events, 66.8 us)
Async XLA Ops:
  7.2 72.1 %copy-start = (bf16[1,256,256]{2,1,0:T(8,128)(2,1)S(1)}, bf16[1,256,256]{2,1,0:T(8,128)(2,1)}, u32[]{:S(2)}) copy-start(bf16[1,256,256]{2,1,0:T(8,128)(2,1)} %param.32) | copy-start | bytes 393220
  8.0 17.5 %copy-start.45 = (s32[128]{0:T(128)}, s32[128]{0:T(128)S(1)}, u32[]{:S(2)}) copy-start(s32[128]{0:T(128)S(1)} %get-tuple-element.188) | copy-start | bytes 1540
  25.5 5.5 %copy-start.38 = (s32[128,128]{1,0:T(8,128)S(1)}, s32[128,128]{1,0:T(8,128)}, u32[]{:S(2)}) copy-start(s32[128,128]{1,0:T(8,128)} %param.35) | copy-start | bytes 196612
  25.6 5.6 %copy-start.50 = (s32[32,1]{0,1:T(1,128)S(1)}, s32[32,1]{0,1:T(1,128)}, u32[]{:S(2)}) copy-start(s32[32,1]{0,1:T(1,128)} %param.37) | copy-start | bytes 388
  25.6 52.5 %copy-start.39 = (bf16[64,256]{1,0:T(8,128)(2,1)S(1)}, bf16[64,256]{1,0:T(8,128)(2,1)}, u32[]{:S(2)}) copy-start(bf16[64,256]{1,0:T(8,128)(2,1)} %param.30) | copy-start | bytes 98308
  25.6 52.5 %copy-start.47 = (f32[256]{0:T(256)S(1)}, f32[256]{0:T(256)}, u32[]{:S(2)}) copy-start(f32[256]{0:T(256)} %param.31) | copy-start | bytes 3076
  25.6 51.8 %all-to-all-start = ((bf16[8,16,64,128]{3,2,1,0:T(8,128)(2,1)}), bf16[8,16,64,128]{3,2,1,0:T(8,128)(2,1)S(1)}, u32[]{:S(2)}, u32[]{:S(2)}) async-start(bf16[8,16,64,128]{3,2,1,0:T(8,128)(2,1)} %bitcast.6), calls=%async_computation | async-start | bytes 4194304 | tf_op jit(solution)/shard_map/all_to_all | solution.py:62
  31.2 48.8 %copy-start.40 = (s32[1024]{0:T(1024)}, s32[1024]{0:T(1024)S(1)}, u32[]{:S(2)}) copy-start(s32[1024]{0:T(1024)S(1)} %pad_clamp_fusion.1) | copy-start | bytes 12292
  31.2 48.8 %copy-start.41 = (pred[32]{0:T(512)(128)(4,1)}, pred[32]{0:T(512)(128)(4,1)S(1)}, u32[]{:S(2)}) copy-start(pred[32]{0:T(512)(128)(4,1)S(1)} %and_bitcast_fusion) | copy-start | bytes 100
  31.2 71.7 %copy-start.20 = (f32[128,1,128]{0,2,1:T(8,128)}, f32[128,1,128]{0,2,1:T(8,128)S(1)}, u32[]{:S(2)}) copy-start(f32[128,1,128]{0,2,1:T(8,128)S(1)} %convert_bitcast_fusion) | copy-start | bytes 196612
  81.3 8.7 %copy-start.51 = (s32[128,1]{0,1:T(1,128)S(1)}, s32[128,1]{0,1:T(1,128)}, u32[]{:S(2)}) copy-start(s32[128,1]{0,1:T(1,128)} %param.36) | copy-start | bytes 1540
  81.3 8.7 %copy-start.32 = (f32[128,4,2,128]{3,2,1,0:T(2,128)S(1)}, f32[128,4,2,128]{3,2,1,0:T(2,128)}, u32[]{:S(2)}) copy-start(f32[128,4,2,128]{3,2,1,0:T(2,128)} %param.27) | copy-start | bytes 1572868
  82.0 13.9 %copy-start.33 = (f32[32,128,2]{1,2,0:T(2,128)}, f32[32,128,2]{1,2,0:T(2,128)S(1)}, u32[]{:S(2)}) copy-start(f32[32,128,2]{1,2,0:T(2,128)S(1)} %fusion.5) | copy-start | bytes 98308
  84.3 11.6 %all-to-all-start.1 = ((bf16[8,16,2,128]{3,2,1,0:T(2,128)(2,1)}), bf16[8,16,2,128]{3,2,1,0:T(2,128)(2,1)S(1)}, u32[]{:S(2)}, u32[]{:S(2)}) async-start(bf16[8,16,2,128]{3,2,1,0:T(2,128)(2,1)} %bitcast.15), calls=%async_computation.1 | async-start | bytes 131072 | tf_op jit(solution)/shard_map/all_to_all | solution.py:76
  96.9 6.0 %copy-start.14 = (f32[128,2,128]{0,2,1:T(8,128)}, f32[128,2,128]{0,2,1:T(8,128)S(1)}, u32[]{:S(2)}) copy-start(f32[128,2,128]{0,2,1:T(8,128)S(1)} %copy.221) | copy-start | bytes 393220
  96.9 2.5 collective-permute-start.1
  97.7 5.2 %collective-permute-start = (f32[128,11,1]{0,2,1:T(1,128)S(1)}, f32[128,11,1]{0,2,1:T(1,128)S(1)}, u32[]{:S(2)}, u32[]{:S(2)}) collective-permute-start(f32[128,11,1]{0,2,1:T(1,128)S(1)} %get-tuple-element.181), channel_id=1, source_target_pairs={{0,4},{4,8},{8,12},{12,16},{16,20},{20,24},{24,28},{28,0},{1,5},{5... | collective-permute-start | bytes 16904 | tf_op jit(solution)/shard_map/ppermute | solution.py:17
  102.9 23.7 %copy-start.37 = (f32[128,11,1]{0,2,1:T(1,128)}, f32[128,11,1]{0,2,1:T(1,128)S(1)}, u32[]{:S(2)}) copy-start(f32[128,11,1]{0,2,1:T(1,128)S(1)} %collective-permute-done) | copy-start | bytes 16900
  103.0 9.4 %copy-start.12 = (f32[128,4,2,128]{3,2,1,0:T(2,128)S(1)}, f32[128,4,2,128]{3,2,1,0:T(2,128)}, u32[]{:S(2)}) copy-start(f32[128,4,2,128]{3,2,1,0:T(2,128)} %param.28) | copy-start | bytes 1572868
  105.9 7.4 %collective-permute-start.3 = (f32[1,11,130]{2,0,1:T(1,128)S(1)}, f32[1,11,130]{2,0,1:T(1,128)}, u32[]{:S(2)}, u32[]{:S(2)}) collective-permute-start(f32[1,11,130]{2,0,1:T(1,128)S(1)} %copy.223), channel_id=1, source_target_pairs={{1,0},{2,1},{3,2},{0,3},{5,4},{6,5},{7,6},{4,7},{9,8},{10,9},{11,1... | collective-permute-start | bytes 17168 | tf_op jit(solution)/shard_map/ppermute | solution.py:20
  111.2 3.2 collective-permute-start.2
  118.3 5.9 %copy-start.1 = (f32[130,8,130]{0,2,1:T(8,128)}, f32[130,8,130]{0,2,1:T(8,128)S(1)}, u32[]{:S(2)}) copy-start(f32[130,8,130]{0,2,1:T(8,128)S(1)} %slice.362) | copy-start | bytes 1622404
  136.0 6.8 %copy-start.29 = (f32[128,129]{0,1:T(8,128)S(1)}, f32[128,129]{0,1:T(8,128)}, u32[]{:S(2)}) copy-start(f32[128,129]{0,1:T(8,128)} %get-tuple-element.156) | copy-start | bytes 198148
  138.2 5.3 %copy-start.16 = (f32[128,2,128]{0,2,1:T(8,128)S(1)}, f32[128,2,128]{0,2,1:T(8,128)}, u32[]{:S(2)}) copy-start(f32[128,2,128]{0,2,1:T(8,128)} %copy-done.14) | copy-start | bytes 393220
  138.2 5.3 %copy-start.22 = (f32[128,1,128]{0,2,1:T(8,128)S(1)}, f32[128,1,128]{0,2,1:T(8,128)}, u32[]{:S(2)}) copy-start(f32[128,1,128]{0,2,1:T(8,128)} %copy-done.20) | copy-start | bytes 196612
  140.5 10.2 %copy-start.13 = (f32[128,4,2,128]{3,2,1,0:T(2,128)S(1)}, f32[128,4,2,128]{3,2,1,0:T(2,128)}, u32[]{:S(2)}) copy-start(f32[128,4,2,128]{3,2,1,0:T(2,128)} %param.28) | copy-start | bytes 1572868
  144.9 5.8 %copy-start.17 = (f32[128,4,2,128]{3,2,1,0:T(2,128)S(1)}, f32[128,4,2,128]{3,2,1,0:T(2,128)}, u32[]{:S(2)}) copy-start(f32[128,4,2,128]{3,2,1,0:T(2,128)} %neg.23) | copy-start | bytes 1572868
  150.7 5.7 %copy-start.27 = (f32[128,129]{1,0:T(8,128)S(1)}, f32[128,129]{1,0:T(8,128)}, u32[]{:S(2)}) copy-start(f32[128,129]{1,0:T(8,128)} %copy.229) | copy-start | bytes 198148
  150.7 5.9 %copy-start.28 = (f32[129,128]{1,0:T(8,128)S(1)}, f32[129,128]{1,0:T(8,128)}, u32[]{:S(2)}) copy-start(f32[129,128]{1,0:T(8,128)} %copy.235) | copy-start | bytes 198148
  150.7 5.9 %copy-start.30 = (f32[129,1,2,128]{3,2,1,0:T(2,128)S(1)}, f32[129,1,2,128]{3,2,1,0:T(2,128)}, u32[]{:S(2)}) copy-start(f32[129,1,2,128]{3,2,1,0:T(2,128)} %copy.269) | copy-start | bytes 396292
  150.7 5.9 %copy-start.31 = (f32[129,1,2,128]{3,2,1,0:T(2,128)S(1)}, f32[129,1,2,128]{3,2,1,0:T(2,128)}, u32[]{:S(2)}) copy-start(f32[129,1,2,128]{3,2,1,0:T(2,128)} %copy.270) | copy-start | bytes 396292
  150.7 6.0 %copy-start.26 = (f32[129,2,128]{2,1,0:T(2,128)S(1)}, f32[129,2,128]{2,1,0:T(2,128)}, u32[]{:S(2)}) copy-start(f32[129,2,128]{2,1,0:T(2,128)} %copy.240) | copy-start | bytes 396292
  199.5 2.5 collective-permute-start.5
  199.6 5.2 %collective-permute-start.4 = (bf16[128,20,1]{0,1,2:T(8,128)(2,1)S(1)}, bf16[128,20,1]{0,1,2:T(8,128)(2,1)S(1)}, u32[]{:S(2)}, u32[]{:S(2)}) collective-permute-start(bf16[128,20,1]{0,1,2:T(8,128)(2,1)S(1)} %get-tuple-element.174), channel_id=1, source_target_pairs={{0,4},{4,8},{8,12},{12,16},{16,20},{20,24},{24,28},{28,0},{1,5},{5... | collective-permute-start | bytes 15368 | tf_op jit(solution)/shard_map/ppermute | solution.py:17
  202.0 24.5 %copy-start.35 = (bf16[128,20,1]{0,1,2:T(8,128)(2,1)}, bf16[128,20,1]{0,1,2:T(8,128)(2,1)S(1)}, u32[]{:S(2)}) copy-start(bf16[128,20,1]{0,1,2:T(8,128)(2,1)S(1)} %collective-permute-done.5) | copy-start | bytes 15364
  204.8 21.7 %copy-start.36 = (bf16[128,20,1]{0,1,2:T(8,128)(2,1)}, bf16[128,20,1]{0,1,2:T(8,128)(2,1)S(1)}, u32[]{:S(2)}) copy-start(bf16[128,20,1]{0,1,2:T(8,128)(2,1)S(1)} %collective-permute-done.4) | copy-start | bytes 15364
  209.6 10.9 %collective-permute-start.7 = (bf16[1,20,130]{2,1,0:T(8,128)(2,1)S(1)}, bf16[1,20,130]{2,1,0:T(8,128)(2,1)S(1)}, u32[]{:S(2)}, u32[]{:S(2)}) collective-permute-start(bf16[1,20,130]{2,1,0:T(8,128)(2,1)S(1)} %copy.246), channel_id=1, source_target_pairs={{1,0},{2,1},{3,2},{0,3},{5,4},{6,5},{7,6},{4,7},{9,8},{10,9},{11,1... | collective-permute-start | bytes 15608 | tf_op jit(solution)/shard_map/ppermute | solution.py:20
  212.7 9.3 %collective-permute-start.6 = (bf16[1,20,130]{2,1,0:T(8,128)(2,1)S(1)}, bf16[1,20,130]{2,1,0:T(8,128)(2,1)S(1)}, u32[]{:S(2)}, u32[]{:S(2)}) collective-permute-start(bf16[1,20,130]{2,1,0:T(8,128)(2,1)S(1)} %copy.245), channel_id=1, source_target_pairs={{0,1},{1,2},{2,3},{3,0},{4,5},{5,6},{6,7},{7,4},{8,9},{9,10},{10,1... | collective-permute-start | bytes 15608 | tf_op jit(solution)/shard_map/ppermute | solution.py:17
  229.0 4.2 copy-start.3
  229.0 4.2 copy-start.5
  235.7 14.0 %copy-start.46 = (s32[128]{0:T(128)S(1)}, s32[128]{0:T(128)}, u32[]{:S(2)}) copy-start(s32[128]{0:T(128)} %copy-done.45) | copy-start | bytes 1540
  247.8 23.1 %copy-start.9 = (f32[128,10,128]{0,1,2:T(8,128)S(1)}, f32[128,10,128]{0,1,2:T(8,128)}, u32[]{:S(2)}) copy-start(f32[128,10,128]{0,1,2:T(8,128)} %scatter-add.19) | copy-start | bytes 1966084
  264.0 9.6 %all-to-all-start.2 = ((bf16[8,16,2,128]{3,2,1,0:T(2,128)(2,1)}), bf16[8,16,2,128]{3,2,1,0:T(2,128)(2,1)S(1)}, u32[]{:S(2)}, u32[]{:S(2)}) async-start(bf16[8,16,2,128]{3,2,1,0:T(2,128)(2,1)} %bitcast.26), calls=%async_computation.2 | async-start | bytes 131072 | tf_op jit(solution)/shard_map/all_to_all | solution.py:62
  267.4 183.4 %all-reduce.23.cloned.1.call-start = ((), (), s32[]{:S(2)}) async-start(), calls=%async_computation.3 | async-start | bytes 655360 | tf_op jit(solution)/shard_map/psum | solution.py:198
  267.5 6.9 %copy-start.34 = (f32[32,128,2]{1,2,0:T(2,128)S(1)}, f32[32,128,2]{1,2,0:T(2,128)}, u32[]{:S(2)}) copy-start(f32[32,128,2]{1,2,0:T(2,128)} %copy-done.33) | copy-start | bytes 98308
  267.5 6.9 %copy-start.42 = (pred[32]{0:T(512)(128)(4,1)S(1)}, pred[32]{0:T(512)(128)(4,1)}, u32[]{:S(2)}) copy-start(pred[32]{0:T(512)(128)(4,1)} %copy-done.41) | copy-start | bytes 100
  267.5 6.9 %copy-start.44 = (f32[2]{0:T(128)S(1)}, f32[2]{0:T(128)}, u32[]{:S(2)}) copy-start(f32[2]{0:T(128)} %param.34) | copy-start | bytes 28
  267.5 7.1 %copy-start.49 = (bf16[256,2]{0,1:T(2,128)(2,1)S(1)}, bf16[256,2]{0,1:T(2,128)(2,1)}, u32[]{:S(2)}) copy-start(bf16[256,2]{0,1:T(2,128)(2,1)} %param.33) | copy-start | bytes 3076
  (16 other events, 24.3 us)
Sparse Core Ops, SparseCore 0:
  323.6 127.1 all-reduce.22
where the time goes:
time: 465 us; the launch traced here: 461 us
  waiting for transfers between devices  187 us (40%)
  local copies, waits for them, and re-layouts  130 us (28%)
  other arithmetic  55.2 us (12%)
  blocking collectives  40 us (9%)
  starting transfers between devices  24.5 us (5%)
  between operations  14.7 us (3%)
  matrix products  9.49 us (2%)
    psum x1, waiting for transfers between devices, on_device(): lax.psum((local_terms[0], local_terms[1], local_terms[2], local_terms[3],...  127 us
    all_to_all x2, waiting for transfers between devices, to_owners(): lax.all_to_all(buffer, 'lon', split_axis=0, concat_axis=0, tiled=True)  46.2 us
    psum x1, blocking collectives, on_device(): lax.psum((local_terms[0], local_terms[1], local_terms[2], local_terms[3],...  40 us
    scatter x2, local copies, waits for them, and re-layouts, to_owners(): jnp.zeros(blocks.shape, blocks.dtype).at[target].set(blocks, mode='drop')  30 us
    unnamed x116, local copies, waits for them, and re-layouts  22.1 us
    scatter x2, local copies, waits for them, and re-layouts, on_device(): lat_rims = jnp.zeros_like(interior).at[0].set(grads_wide[0, :, 1:-1]).at[...  13.2 us
    scatter-add x1, local copies, waits for them, and re-layouts, on_device(): summed = summed.at[-1].add(returned[-1, channels:, 1:-1])  12 us
  transfers between devices with their start and end apart: 12, of which 7 were waited for; matrix products, arithmetic and copies ran while one was open for 5% of the time, Pallas kernels for 0%

commit v1 on v0

v1 whole, which is shorter than its diff:
```python
import functools
import math

import jax
import jax.numpy as jnp
from jax import lax
from jax.experimental import pallas as pl
from jax.experimental.pallas import tpu as pltpu
from jax.sharding import PartitionSpec as P

kappa_most = 0.2
GROUP = 4
CHUNK = 16
F32 = jnp.float32
BF16 = jnp.bfloat16
EXACT = lax.Precision.HIGHEST
NT = (((1,), (1,)), ((), ()))
TN = (((0,), (0,)), ((), ()))


def lane_of(shape):
    return lax.broadcasted_iota(jnp.int32, shape, len(shape) - 1)


def edge_picker(width):
    rows = lax.broadcasted_iota(jnp.int32, (8, width), 0)
    lanes = lax.broadcasted_iota(jnp.int32, (8, width), 1)
    hit = ((rows == 0) & (lanes == 0)) | ((rows == 1) & (lanes == width - 1))
    return hit.astype(F32)


def spread_edges(halo, width):
    return lax.dot_general(
        halo, edge_picker(width), TN, precision=EXACT, preferred_element_type=F32
    )


def pack_edges(values):
    return lax.dot_general(
        edge_picker(values.shape[1]), values, NT, precision=EXACT, preferred_element_type=F32
    )


def between(west, east):
    return jnp.concatenate([west[1:2], east[0:1], jnp.zeros((6, west.shape[1]), F32)], axis=0)


def ring(axis, step):
    count = lax.axis_size(axis)
    return lax.rem(lax.axis_index(axis) + (step + count), count)


def push(source, target, sems, index, axis, step):
    send, recv = sems
    copy = pltpu.make_async_remote_copy(
        src_ref=source,
        dst_ref=target,
        send_sem=send.at[index],
        recv_sem=recv.at[index],
        device_id={axis: ring(axis, step)},
        device_id_type=pl.DeviceIdType.MESH,
    )
    copy.start()
    return copy


def greet(peers):
    barrier = pltpu.get_barrier_semaphore()
    for axis, step in peers:
        pl.semaphore_signal(
            barrier,
            inc=1,
            device_id={axis: ring(axis, step)},
            device_id_type=pl.DeviceIdType.MESH,
        )
    pl.semaphore_wait(barrier, len(peers))


def halo_kernel(
    state_ref,
    cot_ref,
    sea_ref,
    home_ref,
    list_ref,
    flags_ref,
    state_edge_ref,
    cot_edge_ref,
    sea_edge_ref,
    state_rows_ref,
    cot_rows_ref,
    sea_rows_ref,
    lists,
    edge_out,
    edge_in,
    rows_out,
    rows_in,
    list_send,
    list_recv,
    halo_send,
    halo_recv,
):
    rows, subs, width = state_ref.shape
    span = rows * subs
    lon_count = lax.axis_size("lon")
    cap = rows // lon_count
    lat_index = lax.axis_index("lat")
    peers = [("lon", d) for d in range(1, lon_count)] + [("lat", 1), ("lat", -1)]
    greet(peers)
    copies = []
    for d in range(1, lon_count):
        copies.append(push(list_ref, lists.at[d], (list_send, list_recv), d, "lon", d))
    for side, row in ((0, 0), (1, rows - 1)):
        rows_out[side, 0:subs] = state_ref[row]
        rows_out[side, subs : 2 * subs] = cot_ref[row]
        rows_out[side, 2 * subs : 2 * subs + 8] = jnp.broadcast_to(
            sea_ref[row : row + 1], (8, width)
        )
    halo = (halo_send, halo_recv)
    copies.append(push(rows_out.at[0], rows_in.at[1], halo, 0, "lat", -1))
    copies.append(push(rows_out.at[1], rows_in.at[0], halo, 1, "lat", 1))
    edge_out[:, 0:span] = pack_edges(state_ref[...].reshape(span, width))
    edge_out[:, span : 2 * span] = pack_edges(cot_ref[...].reshape(span, width))
    edge_out[:, 2 * span :] = pack_edges(sea_ref[...])
    copies.append(push(edge_out, edge_in.at[1], halo, 2, "lon", -1))
    copies.append(push(edge_out, edge_in.at[0], halo, 3, "lon", 1))
    for copy in copies:
        copy.wait()

    me = lax.axis_index("lon")
    home = home_ref[...]
    found = jnp.zeros(list_ref.shape, jnp.int32)
    for d in range(lon_count):
        entries = list_ref[...] if d == 0 else lists[d]
        owner = ring("lon", -d)
        source = entries // cap
        wanted = owner * cap + (entries - source * cap)
        hit = (source == me) & (wanted == home)
        found = jnp.where(hit, 1, found)
    flags_ref[...] = jnp.max(found, axis=0, keepdims=True)
    edges = between(edge_in[0], edge_in[1])
    state_edge_ref[...] = edges[:, 0:span]
    cot_edge_ref[...] = edges[:, span : 2 * span]
    sea_edge_ref[...] = edges[:, 2 * span :]
    inside = (lat_index > 0, lat_index < lax.axis_size("lat") - 1)
    state_rows_ref[...] = rows_in[:, 0:subs]
    cot_rows_ref[...] = rows_in[:, subs : 2 * subs]
    for side in range(2):
        open_here = jnp.where(inside[side], 1.0, 0.0)
        sea_rows_ref[side : side + 1] = rows_in[side, 2 * subs : 2 * subs + 1] * open_here
    sea_rows_ref[2:8] = jnp.zeros((6, width), F32)


def west_of(values, edge):
    rolled = pltpu.roll(values, 1, values.ndim - 1)
    return jnp.where(lane_of(values.shape) == 0, edge, rolled)


def east_of(values, edge):
    width = values.shape[-1]
    rolled = pltpu.roll(values, width - 1, values.ndim - 1)
    return jnp.where(lane_of(values.shape) == width - 1, edge, rolled)


def field_sum(values):
    values = values + pltpu.roll(values, 2, 1)
    return values + pltpu.roll(values, 4, 1)


def repeat_field(values, field):
    sub = lax.broadcasted_iota(jnp.int32, values.shape, 1)
    picked = jnp.where(sub // 2 == field, values, 0.0)
    return field_sum(picked)


def padded_load(ref, edges, start, size, total, offset):
    middle = ref[pl.ds(start, size)]
    if offset < 0:
        below = ref[pl.ds(jnp.maximum(start - 1, 0), 1)]
        below = jnp.where(start == 0, edges[0:1], below)
        return jnp.concatenate([below, middle[:-1]], axis=0)
    above = ref[pl.ds(jnp.minimum(start + size, total - 1), 1)]
    above = jnp.where(start + size >= total, edges[1:2], above)
    return jnp.concatenate([middle[1:], above], axis=0)


def prepare_sea(sea_ref, sea_edge_ref, sea_rows_ref, open_refs):
    rows, width = sea_ref.shape
    sea = sea_ref[...]
    edge = spread_edges(sea_edge_ref[...], width)
    south = jnp.concatenate([sea_rows_ref[0:1], sea[:-1]], axis=0)
    north = jnp.concatenate([sea[1:], sea_rows_ref[1:2]], axis=0)
    for ref, other in zip(open_refs, (west_of(sea, edge), east_of(sea, edge), south, north)):
        ref[...] = sea * other


def closure_kernel(
    flags_ref,
    features_ref,
    state_ref,
    cot_ref,
    sea_ref,
    state_edge_ref,
    cot_edge_ref,
    sea_edge_ref,
    state_rows_ref,
    cot_rows_ref,
    sea_rows_ref,
    w_in_ref,
    w_mid_ref,
    small_ref,
    bias_out_ref,
    diff_ref,
    diff_edge_ref,
    sums_ref,
    open_w,
    open_e,
    open_s,
    open_n,
    state_x,
    cot_x,
    kgrad,
    w_in_t,
    w_mid_t,
    bias_in_col,
    w_out_rep,
    w_out_col,
    acc_in,
    acc_mid,
    acc_out,
    acc_bias,
    acc_bout,
    order,
):
    rows, subs, width = state_ref.shape
    hid = w_mid_ref.shape[0]

    def note(row, count):
        order[count] = row
        return count + flags_ref[row]

    count = lax.fori_loop(0, rows, note, jnp.int32(0))
    for extra in range(GROUP):
        order[count + extra] = rows

    prepare_sea(sea_ref, sea_edge_ref, sea_rows_ref, (open_w, open_e, open_s, open_n))
    state_x[...] = spread_edges(state_edge_ref[...], width).reshape(rows, subs, width)
    cot_x[...] = spread_edges(cot_edge_ref[...], width).reshape(rows, subs, width)

    def kappa_chunk(step, carry):
        start = pl.multiple_of(step * CHUNK, CHUNK)
        at = pl.ds(start, CHUNK)
        q = state_ref[at]
        g = cot_ref[at]
        qx = state_x[at]
        gx = cot_x[at]

        def part(opened, q_near, g_near):
            return (g_near - g) * (q_near - q) * opened[at][:, None, :]

        total = part(open_w, west_of(q, qx), west_of(g, gx))
        total += part(open_e, east_of(q, qx), east_of(g, gx))
        total += part(
            open_s,
            padded_load(state_ref, state_rows_ref, start, CHUNK, rows, -1),
            padded_load(cot_ref, cot_rows_ref, start, CHUNK, rows, -1),
        )
        total += part(
            open_n,
            padded_load(state_ref, state_rows_ref, start, CHUNK, rows, 1),
            padded_load(cot_ref, cot_rows_ref, start, CHUNK, rows, 1),
        )
        kgrad[at] = field_sum(total) * -0.5
        diff_ref[at] = jnp.zeros((CHUNK, subs, width), F32)
        return carry

    lax.fori_loop(0, rows // CHUNK, kappa_chunk, 0)
    kgrad[pl.ds(rows, 8)] = jnp.zeros((8, subs, width), F32)

    small_t = small_ref[...].T
    bias_in_col[...] = jnp.broadcast_to(small_t[:, 8:9], (hid, width))
    w_out_rep[...] = small_ref[0:8].astype(BF16)
    w_out_col[...] = jnp.where(lane_of((hid, 8)) < 2, small_t[:, 0:8], 0.0).astype(BF16)
    w_in_t[...] = w_in_ref[...].astype(F32).T.astype(BF16)
    w_mid_t[...] = w_mid_ref[...].astype(F32).T.astype(BF16)
    for ref in (acc_in, acc_mid, acc_out, acc_bias, acc_bout):
        ref[...] = jnp.zeros(ref.shape, F32)

    def group(step, carry):
        picked = [order[step * GROUP + i] for i in range(GROUP)]
        loads = [jnp.minimum(row, rows - 1) for row in picked]
        x = jnp.concatenate([features_ref[row] for row in loads], axis=1)
        kap = jnp.concatenate([kgrad[row] for row in picked], axis=1)
        bias_in = jnp.concatenate([bias_in_col[...]] * GROUP, axis=1)
        first = jnp.dot(w_in_t[...], x, preferred_element_type=F32) + bias_in
        h0 = jnp.tanh(first).astype(BF16)
        h1 = jnp.tanh(jnp.dot(w_mid_t[...], h0, preferred_element_type=F32)).astype(BF16)
        logits = jnp.dot(w_out_rep[...], h1, preferred_element_type=F32)
        logits = logits + jnp.concatenate([bias_out_ref[...]] * GROUP, axis=1)
        squashed = 1.0 / (1.0 + jnp.exp(-logits))
        for i, row in enumerate(picked):
            diff_ref[row] = kappa_most * squashed[:, i * width : (i + 1) * width]
        kap_low = kap.astype(BF16).astype(F32)
        logit_grad = kap_low * (kappa_most * squashed * (1.0 - squashed))
        logit_low = logit_grad.astype(BF16)
        acc_out[...] += lax.dot_general(logit_low, h1, NT, preferred_element_type=F32)
        acc_bout[...] += functools.reduce(
            jnp.add, [logit_grad[:, i * width : (i + 1) * width] for i in range(GROUP)]
        )
        carried = jnp.dot(w_out_col[...], logit_low, preferred_element_type=F32)
        current = h1.astype(F32)
        layer_grad = (carried * (1.0 - current * current)).astype(BF16)
        acc_mid[...] += lax.dot_general(h0, layer_grad, NT, preferred_element_type=F32)
        carried = jnp.dot(w_mid_ref[...], layer_grad, preferred_element_type=F32)
        base = h0.astype(F32)
        first_grad = carried * (1.0 - base * base)
        acc_bias[...] += functools.reduce(
            jnp.add, [first_grad[:, i * width : (i + 1) * width] for i in range(GROUP)]
        )
        acc_in[...] += lax.dot_general(
            x, first_grad.astype(BF16), NT, preferred_element_type=F32
        )
        return carry

    lax.fori_loop(0, (count + GROUP - 1) // GROUP, group, 0)

    scaling = 1.0 / math.sqrt(rows * width)
    f_in = w_in_ref.shape[0]
    ones = jnp.ones((8, width), F32)
    row_bias = lax.dot_general(ones, acc_bias[...], NT, precision=EXACT, preferred_element_type=F32)
    tall = jnp.concatenate([acc_bout[...], jnp.zeros((hid - 8, width), F32)], axis=0)
    row_bout = lax.dot_general(ones, tall, NT, precision=EXACT, preferred_element_type=F32)
    which = lax.broadcasted_iota(jnp.int32, (8, hid), 0)
    misc = jnp.where(which < 2, acc_out[...], jnp.where(which == 2, row_bias, row_bout))
    misc = jnp.where(which < 4, misc, 0.0)
    diff_edge_ref[...] = pack_edges(diff_ref[0:rows].reshape(rows * subs, width))
    tiles = 0
    for block in (acc_mid[...], acc_in[...], misc):
        for half in range(hid // width):
            count = block.shape[0] // 8
            part = block[:, half * width : (half + 1) * width] * scaling
            sums_ref[tiles : tiles + count] = part.reshape(count, 8, width)
            tiles += count
    spare = sums_ref.shape[0] - tiles
    if spare:
        sums_ref[tiles : tiles + spare] = jnp.zeros((spare, 8, width), F32)


def stencil_kernel(
    state_ref,
    cot_ref,
    sea_ref,
    diff_ref,
    state_edge_ref,
    cot_edge_ref,
    sea_edge_ref,
    diff_edge_ref,
    state_rows_ref,
    cot_rows_ref,
    sea_rows_ref,
    sums_ref,
    new_ref,
    adj_ref,
    grad_in_ref,
    grad_bias_in_ref,
    grad_mid_ref,
    grad_out_ref,
    grad_bias_out_ref,
    open_w,
    open_e,
    open_s,
    open_n,
    state_x,
    cot_x,
    diff_x,
    diff_rows_ref,
    edge_in,
    from_lat,
    for_lon,
    from_lon,
    chunk_sum,
    gathered,
    full,
    halo_send,
    halo_recv,
    lat_send,
    lat_recv,
    lon_send,
    lon_recv,
):
    rows, subs, width = state_ref.shape
    lat_count, lon_count = sums_ref.shape[:2]
    lat_me = lax.axis_index("lat")
    lon_me = lax.axis_index("lon")
    lat_steps = range(1, lat_count)
    lon_steps = range(1, lon_count)
    greet([("lon", d) for d in lon_steps] + [("lat", d) for d in lat_steps])
    halo = (halo_send, halo_recv)
    halo_copies = [
        push(diff_ref.at[0], diff_rows_ref.at[1], halo, 0, "lat", -1),
        push(diff_ref.at[rows - 1], diff_rows_ref.at[0], halo, 1, "lat", 1),
        push(diff_edge_ref, edge_in.at[1], halo, 2, "lon", -1),
        push(diff_edge_ref, edge_in.at[0], halo, 3, "lon", 1),
    ]
    lat_sems = (lat_send, lat_recv)
    lon_sems = (lon_send, lon_recv)
    reduce_lat = [
        push(sums_ref.at[ring("lat", d)], from_lat.at[d], lat_sems, d, "lat", d) for d in lat_steps
    ]
    prepare_sea(sea_ref, sea_edge_ref, sea_rows_ref, (open_w, open_e, open_s, open_n))
    state_x[...] = spread_edges(state_edge_ref[...], width).reshape(rows, subs, width)
    cot_x[...] = spread_edges(cot_edge_ref[...], width).reshape(rows, subs, width)
    for copy in halo_copies:
        copy.wait()
    diff_x[...] = spread_edges(between(edge_in[0], edge_in[1]), width).reshape(rows, subs, width)

    def chunk(step, carry):
        start = pl.multiple_of(step * CHUNK, CHUNK)
        at = pl.ds(start, CHUNK)
        q = state_ref[at]
        g = cot_ref[at]
        k = diff_ref[at]
        sub = lax.broadcasted_iota(jnp.int32, q.shape, 1)

        def face(sign, field, opened, q_near, g_near, k_near):
            gate = opened[at][:, None, :]
            speed = repeat_field(q + q_near, field) * (0.5 * gate)
            kf = (k + k_near) * (0.5 * gate)
            q_sum = 0.5 * (q + q_near)
            g_diff = g_near - g
            new_part = kf * (q_near - q) - sign * speed * q_sum
            w_part = field_sum(g_diff * q_sum) * ((0.5 * sign) * gate)
            adj_part = g_diff * (kf + (0.5 * sign) * speed)
            adj_part = adj_part + jnp.where(sub // 2 == field, w_part, 0.0)
            return new_part, adj_part

        qx, gx, kx = state_x[at], cot_x[at], diff_x[at]
        parts = [
            face(-1.0, 2, open_w, west_of(q, qx), west_of(g, gx), west_of(k, kx)),
            face(1.0, 2, open_e, east_of(q, qx), east_of(g, gx), east_of(k, kx)),
        ]
        for sign, offset, opened in ((-1.0, -1, open_s), (1.0, 1, open_n)):
            parts.append(
                face(
                    sign,
                    3,
                    opened,
                    padded_load(state_ref, state_rows_ref, start, CHUNK, rows, offset),
                    padded_load(cot_ref, cot_rows_ref, start, CHUNK, rows, offset),
                    padded_load(diff_ref, diff_rows_ref, start, CHUNK, rows, offset),
                )
            )
        new_ref[at] = q + parts[0][0] + parts[1][0] + parts[2][0] + parts[3][0]
        adj_ref[at] = g + parts[0][1] + parts[1][1] + parts[2][1] + parts[3][1]
        return carry

    steps = rows // CHUNK
    lax.fori_loop(0, steps // 2, chunk, 0)
    for copy in reduce_lat:
        copy.wait()
    total = sums_ref[lat_me]
    for d in lat_steps:
        total = total + from_lat[d]
    for_lon[...] = total
    reduce_lon = [
        push(for_lon.at[ring("lon", d)], from_lon.at[d], lon_sems, d, "lon", d) for d in lon_steps
    ]
    lax.fori_loop(steps // 2, steps, chunk, 0)
    for copy in reduce_lon:
        copy.wait()
    total = for_lon[lon_me]
    for d in lon_steps:
        total = total + from_lon[d]
    chunk_sum[...] = total
    gathered[lon_me] = total
    spread_lon = [
        push(chunk_sum, gathered.at[lon_me], lon_sems, lon_count + d, "lon", d) for d in lon_steps
    ]
    for copy in spread_lon:
        copy.wait()
    spread_lat = [
        push(gathered, full.at[lat_me], lat_sems, lat_count + d, "lat", d) for d in lat_steps
    ]
    full[lat_me] = gathered[...]
    for copy in spread_lat:
        copy.wait()

    hid = grad_mid_ref.shape[0]
    flat = full[...].reshape(lat_count * lon_count * full.shape[2], 8, width)
    tiles = 0
    halves = hid // width
    for ref in (grad_mid_ref, grad_in_ref):
        count = ref.shape[0] // 8
        for half in range(halves):
            ref[:, half * width : (half + 1) * width] = flat[tiles : tiles + count].reshape(
                8 * count, width
            )
            tiles += count
    misc = jnp.concatenate([flat[tiles + half] for half in range(halves)], axis=1)
    levels = grad_out_ref.shape[1]
    grad_bias_in_ref[...] = misc[2:3]
    grad_bias_out_ref[...] = misc[3:4, 0:levels]
    grad_out_ref[...] = misc.T[:, 0:levels]


def on_device(
    ocean_state,
    cotangent,
    features,
    w_in,
    bias_in,
    w_mid,
    w_out,
    bias_out,
    land_mask,
    home_slot,
    owner_list,
):
    rows, fields, levels, width = ocean_state.shape
    subs = fields * levels
    f_in, hid = w_in.shape
    lon_count = lax.axis_size("lon")
    lat_count = lax.axis_size("lat")

    state = ocean_state.reshape(rows, subs, width)
    cot = cotangent.reshape(rows, subs, width)
    sea = land_mask.astype(F32)
    span = rows * subs
    vmem = pl.BlockSpec(memory_space=pltpu.VMEM)
    smem = pl.BlockSpec(memory_space=pltpu.SMEM)
    dma = pltpu.SemaphoreType.DMA
    listed = owner_list.shape[0]
    flags, state_edge, cot_edge, sea_edge, state_rows, cot_rows, sea_rows = pl.pallas_call(
        halo_kernel,
        name="halo",
        out_shape=(
            jax.ShapeDtypeStruct((1, rows), jnp.int32),
            jax.ShapeDtypeStruct((8, span), F32),
            jax.ShapeDtypeStruct((8, span), F32),
            jax.ShapeDtypeStruct((8, rows), F32),
            jax.ShapeDtypeStruct((2, subs, width), F32),
            jax.ShapeDtypeStruct((2, subs, width), F32),
            jax.ShapeDtypeStruct((8, width), F32),
        ),
        in_specs=[vmem] * 5,
        out_specs=(vmem,) * 7,
        scratch_shapes=[
            pltpu.VMEM((lon_count, listed, rows), jnp.int32),
            pltpu.VMEM((8, 2 * span + rows), F32),
            pltpu.VMEM((2, 8, 2 * span + rows), F32),
            pltpu.VMEM((2, 2 * subs + 8, width), F32),
            pltpu.VMEM((2, 2 * subs + 8, width), F32),
            dma((lon_count,)),
            dma((lon_count,)),
            dma((4,)),
            dma((4,)),
        ],
        compiler_params=pltpu.CompilerParams(
            collective_id=0, has_side_effects=True, vmem_limit_bytes=32 * 1024 * 1024
        ),
    )(
        state,
        cot,
        sea,
        home_slot.reshape(1, rows),
        jnp.broadcast_to(owner_list, (listed, rows)),
    )
    flags = flags.reshape(rows)

    small = jnp.concatenate(
        [
            jnp.tile(w_out.astype(F32).T, (8 // levels, 1)),
            bias_in[None],
            jnp.zeros((7, hid), F32),
        ],
        axis=0,
    )
    bias_out_rep = jnp.broadcast_to(jnp.tile(bias_out, (8 // levels,))[:, None], (8, width))

    tiles = (hid // width) * (hid + f_in + 8) // 8
    share = -(-tiles // (lat_count * lon_count))
    mask = pltpu.VMEM((rows, width), F32)
    slab = pltpu.VMEM((rows, subs, width), F32)
    diff, diff_edge, sums = pl.pallas_call(
        closure_kernel,
        name="closure",
        out_shape=(
            jax.ShapeDtypeStruct((rows + 8, subs, width), F32),
            jax.ShapeDtypeStruct((8, span), F32),
            jax.ShapeDtypeStruct((lat_count * lon_count * share, 8, width), F32),
        ),
        in_specs=[smem] + [vmem] * 14,
        out_specs=(vmem,) * 3,
        scratch_shapes=[
            mask,
            mask,
            mask,
            mask,
            slab,
            slab,
            pltpu.VMEM((rows + 8, subs, width), F32),
            pltpu.VMEM((hid, f_in), BF16),
            pltpu.VMEM((hid, hid), BF16),
            pltpu.VMEM((hid, width), F32),
            pltpu.VMEM((8, hid), BF16),
            pltpu.VMEM((hid, 8), BF16),
            pltpu.VMEM((f_in, hid), F32),
            pltpu.VMEM((hid, hid), F32),
            pltpu.VMEM((8, hid), F32),
            pltpu.VMEM((hid, width), F32),
            pltpu.VMEM((8, width), F32),
            pltpu.SMEM((rows + 2 * GROUP,), jnp.int32),
        ],
        compiler_params=pltpu.CompilerParams(vmem_limit_bytes=40 * 1024 * 1024),
    )(
        flags,
        features,
        state,
        cot,
        sea,
        state_edge,
        cot_edge,
        sea_edge,
        state_rows,
        cot_rows,
        sea_rows,
        w_in,
        w_mid[0],
        small,
        bias_out_rep,
    )

    piece = (share, 8, width)
    new_state, adjoint, grad_in, grad_bias_in, grad_mid, grad_out, grad_bias_out = pl.pallas_call(
        stencil_kernel,
        name="stencil",
        out_shape=(
            jax.ShapeDtypeStruct((rows, subs, width), F32),
            jax.ShapeDtypeStruct((rows, subs, width), F32),
            jax.ShapeDtypeStruct((f_in, hid), F32),
            jax.ShapeDtypeStruct((1, hid), F32),
            jax.ShapeDtypeStruct((hid, hid), F32),
            jax.ShapeDtypeStruct((hid, levels), F32),
            jax.ShapeDtypeStruct((1, levels), F32),
        ),
        in_specs=[vmem] * 12,
        out_specs=(vmem,) * 7,
        scratch_shapes=[
            mask,
            mask,
            mask,
            mask,
            slab,
            slab,
            slab,
            pltpu.VMEM((2, subs, width), F32),
            pltpu.VMEM((2, 8, span), F32),
            pltpu.VMEM((lat_count, lon_count) + piece, F32),
            pltpu.VMEM((lon_count,) + piece, F32),
            pltpu.VMEM((lon_count,) + piece, F32),
            pltpu.VMEM(piece, F32),
            pltpu.VMEM((lon_count,) + piece, F32),
            pltpu.VMEM((lat_count, lon_count) + piece, F32),
            dma((4,)),
            dma((4,)),
            dma((2 * lat_count,)),
            dma((2 * lat_count,)),
            dma((2 * lon_count,)),
            dma((2 * lon_count,)),
        ],
        compiler_params=pltpu.CompilerParams(
            collective_id=1, has_side_effects=True, vmem_limit_bytes=32 * 1024 * 1024
        ),
    )(
        state,
        cot,
        sea,
        diff,
        state_edge,
        cot_edge,
        sea_edge,
        diff_edge,
        state_rows,
        cot_rows,
        sea_rows,
        sums.reshape((lat_count, lon_count) + piece),
    )
    return (
        new_state.reshape(ocean_state.shape),
        adjoint.reshape(ocean_state.shape),
        grad_in,
        grad_bias_in[0],
        grad_mid[None],
        grad_out,
        grad_bias_out[0],
    )


def solution(mesh):
    in_specs = (
        P("lat", None, None, "lon"),
        P("lat", None, None, "lon"),
        P("lat", None, "lon"),
        P(),
        P(),
        P(),
        P(),
        P(),
        P("lat", "lon"),
        P("lat", "lon"),
        P("lat", "lon"),
    )
    out_specs = (P("lat", None, None, "lon"), P("lat", None, None, "lon"), P(), P(), P(), P(), P())
    return jax.shard_map(
        on_device, mesh=mesh, in_specs=in_specs, out_specs=out_specs, check_vma=False
    )
```

time: 465 us -> 77 us (0.17)
  waiting for transfers between devices: 187 us -> 0 us
  local copies, waits for them, and re-layouts: 130 us -> 14.3 us
  Pallas kernels: 0 us -> 60.1 us
  other arithmetic: 55.2 us -> 2.28 us
  blocking collectives: 40 us -> 0 us
  starting transfers between devices: 24.5 us -> 0 us
  between operations: 14.7 us -> 0.68 us
  matrix products: 9.49 us -> 0 us
    psum x1 -> x0, waiting for transfers between devices: 127 us -> none  [on_device(): lax.psum((local_terms[0], local_terms[1], local_terms[2], local_terms[3],...]
    pallas_call x0 -> x3, Pallas kernels: none -> 60.1 us  [the longest x1 43.3 us: on_device(): pl.pallas_call(stencil_kernel, name='stencil', out_shape=(jax.ShapeDtypeS...]
    all_to_all x3 -> x0, waiting for transfers between devices: 51.6 us -> none  [the longest x2 46.2 us: to_owners(): lax.all_to_all(buffer, 'lon', split_axis=0, concat_axis=0, tiled=True)]
    scatter x6 -> x0, local copies, waits for them, and re-layouts: 45.6 us -> none  [the longest x2 30 us: to_owners(): jnp.zeros(blocks.shape, blocks.dtype).at[target].set(blocks, mode='drop')]
    psum x1 -> x0, blocking collectives: 40 us -> none  [on_device(): lax.psum((local_terms[0], local_terms[1], local_terms[2], local_terms[3],...]
    slice x15 -> x0, local copies, waits for them, and re-layouts: 19.6 us -> none  [the longest x4 6.84 us: with_halo(): lax.slice_in_dim(block, block.shape[dim] - width, None, axis=dim)]
    scatter-add x2 -> x0, local copies, waits for them, and re-layouts: 16.2 us -> none  [the longest x1 12 us: on_device(): summed = summed.at[-1].add(returned[-1, channels:, 1:-1])]
    all_to_all x3 -> x0, starting transfers between devices: 14.5 us -> none  [the longest x2 8.84 us: to_owners(): lax.all_to_all(buffer, 'lon', split_axis=0, concat_axis=0, tiled=True)]
  transfers between devices with their start and end apart: 12 -> 0, of which waited for: 7 -> 0; matrix products, arithmetic and copies ran while one was open for 5% -> 0% of each run, Pallas kernels for 0% -> 0%
where the time goes in v1:
time: 77 us; the launch traced here: 77.4 us
  Pallas kernels  60.1 us (78%)
  local copies, waits for them, and re-layouts  14.3 us (19%)
  other arithmetic  2.28 us (3%)
    pallas_call x1, Pallas kernels, on_device(): pl.pallas_call(stencil_kernel, name='stencil', out_shape=(jax.ShapeDtypeS...  43.3 us
    unnamed x23, local copies, waits for them, and re-layouts  12.7 us
    pallas_call x1, Pallas kernels, on_device(): pl.pallas_call(halo_kernel, name='halo', out_shape=(jax.ShapeDtypeStruct(...  12.1 us
    pallas_call x1, Pallas kernels, on_device(): pl.pallas_call(closure_kernel, name='closure', out_shape=(jax.ShapeDtypeS...  4.66 us

profile of v1, /device:TPU:1, one launch (start us, length us, event | category | flops | bytes accessed | tf_op | source)
XLA Modules:
  0.0 77.4 jit_solution(7060617818323759306)
XLA Ops:
  0.6 0.1 pad.2.clone
  0.7 0.7 convert_bitcast_fusion
  1.4 0.7 tile.8
  2.1 0.1 broadcast_in_dim.27
  2.1 0.1 broadcast_in_dim.28.bias_out_ref
  2.2 0.8 maximum_maximum_fusion.small_ref
  3.0 0.7 broadcast_in_dim.24.list_ref
  3.7 0.8 %convert_element_type.4.sea_ref = f32[128,128]{1,0:T(8,128)S(1)} convert(s32[128,128]{1,0:T(8,128)} %param.19) | non-fusion elementwise | flops 16384 | bytes 131072 | tf_op jit(solution)/shard_map/convert_element_type | solution.py:526
  4.6 0.0 copy-start
  4.6 1.0 %copy-done = f32[128,4,2,128]{3,2,1,0:T(2,128)S(1)} copy-done((f32[128,4,2,128]{3,2,1,0:T(2,128)S(1)}, f32[128,4,2,128]{3,2,1,0:T(2,128)}, u32[]{:S(2)}) %copy-start) | copy-done | bytes 524312
  5.6 0.0 copy-start.2
  5.6 1.0 %copy-done.2 = f32[128,4,2,128]{3,2,1,0:T(2,128)S(1)} copy-done((f32[128,4,2,128]{3,2,1,0:T(2,128)S(1)}, f32[128,4,2,128]{3,2,1,0:T(2,128)}, u32[]{:S(2)}) %copy-start.2) | copy-done | bytes 524312
  6.6 0.0 copy-start.7
  6.6 0.7 copy-done.7
  7.3 12.1 %halo.1 = (s32[1,128]{1,0:T(1,128)S(1)}, f32[8,1024]{1,0:T(8,128)S(1)}, f32[8,1024]{1,0:T(8,128)S(1)}, f32[8,128]{1,0:T(8,128)S(1)}, f32[2,8,128]{2,1,0:T(8,128)...) custom-call(f32[128,8,128]{2,1,0:T(8,128)S(1)} %bitcast.15, f32[128,8,128]{2,1,0:T(8,128)S(1)} %bitcast.18, ...), custom_call_target="tpu_custom_call" | custom-call | tf_op jit(solution)/shard_map/halo/pallas_call | solution.py:532
  19.4 0.0 copy-start.1
  19.4 1.0 %copy-done.1 = f32[128,4,2,128]{3,2,1,0:T(2,128)S(1)} copy-done((f32[128,4,2,128]{3,2,1,0:T(2,128)S(1)}, f32[128,4,2,128]{3,2,1,0:T(2,128)}, u32[]{:S(2)}) %copy-start.1) | copy-done | bytes 524312
  20.4 0.0 copy-start.3
  20.4 1.0 %copy-done.3 = f32[128,4,2,128]{3,2,1,0:T(2,128)S(1)} copy-done((f32[128,4,2,128]{3,2,1,0:T(2,128)S(1)}, f32[128,4,2,128]{3,2,1,0:T(2,128)}, u32[]{:S(2)}) %copy-start.3) | copy-done | bytes 524312
  21.5 0.0 copy-start.4
  21.5 1.6 %copy-done.4 = bf16[128,64,128]{2,1,0:T(8,128)(2,1)S(1)} copy-done((bf16[128,64,128]{2,1,0:T(8,128)(2,1)S(1)}, bf16[128,64,128]{2,1,0:T(8,128)(2,1)}, u32[]{:S(2)}) %copy-start.4) | copy-done | bytes 2097176
  23.1 0.0 copy-start.5
  23.1 0.9 %copy-done.5 = bf16[1,256,256]{2,1,0:T(8,128)(2,1)S(1)} copy-done((bf16[1,256,256]{2,1,0:T(8,128)(2,1)S(1)}, bf16[1,256,256]{2,1,0:T(8,128)(2,1)}, u32[]{:S(2)}) %copy-start.5) | copy-done | bytes 131096
  24.0 0.0 copy-start.6
  24.0 0.8 copy-done.6
  24.7 4.7 %closure.1 = (f32[136,8,128]{2,1,0:T(8,128)S(1)}, f32[8,1024]{1,0:T(8,128)S(1)}, f32[96,8,128]{2,1,0:T(8,128)S(1)}) custom-call(s32[128]{0:T(128)S(1)} %bitcast.28, bf16[128,64,128]{2,1,0:T(8,128)(2,1)S(1)} %copy-done.4, f32[128,8,128]{2,1,0:T(8,128)S(1)} %bitcast.16, f32[128,8,128]{2,1,0:T(8,128)S(1)} %bitcast.19, ...), custom_call_target="tpu_custom_call" | custom-call | tf_op jit(solution)/shard_map/closure/pallas_call | solution.py:583
  29.4 43.3 %stencil.1 = (f32[128,8,128]{2,1,0:T(8,128)S(1)}, f32[128,8,128]{2,1,0:T(8,128)S(1)}, f32[64,256]{1,0:T(8,128)S(1)}, f32[1,256]{1,0:T(1,128)S(1)}, f32[256,256]{...) custom-call(f32[128,8,128]{2,1,0:T(8,128)S(1)} %bitcast.17, f32[128,8,128]{2,1,0:T(8,128)S(1)} %bitcast.20, ...), custom_call_target="tpu_custom_call" | custom-call | tf_op jit(solution)/shard_map/stencil/pallas_call | solution.py:633
  72.7 0.7 copy.19
  73.4 0.8 %copy.26 = f32[128,4,2,128]{3,2,1,0:T(2,128)} copy(f32[128,4,2,128]{3,2,1,0:T(2,128)S(1)} %bitcast.22) | data formatting | bytes 1048576
  74.2 0.8 %copy.27 = f32[128,4,2,128]{3,2,1,0:T(2,128)} copy(f32[128,4,2,128]{3,2,1,0:T(2,128)S(1)} %bitcast.21) | data formatting | bytes 1048576
  75.0 0.6 copy.28
  75.6 0.6 copy.29
  76.2 0.7 copy.30
  76.9 0.5 copy.31
  (3 shorter events, 0.0 us)
Async XLA Ops:
  4.6 1.0 %copy-start = (f32[128,4,2,128]{3,2,1,0:T(2,128)S(1)}, f32[128,4,2,128]{3,2,1,0:T(2,128)}, u32[]{:S(2)}) copy-start(f32[128,4,2,128]{3,2,1,0:T(2,128)} %param.11) | copy-start | bytes 1572868
  5.6 1.0 %copy-start.2 = (f32[128,4,2,128]{3,2,1,0:T(2,128)S(1)}, f32[128,4,2,128]{3,2,1,0:T(2,128)}, u32[]{:S(2)}) copy-start(f32[128,4,2,128]{3,2,1,0:T(2,128)} %param.12) | copy-start | bytes 1572868
  6.6 0.7 copy-start.7
  19.4 1.0 %copy-start.1 = (f32[128,4,2,128]{3,2,1,0:T(2,128)S(1)}, f32[128,4,2,128]{3,2,1,0:T(2,128)}, u32[]{:S(2)}) copy-start(f32[128,4,2,128]{3,2,1,0:T(2,128)} %param.11) | copy-start | bytes 1572868
  20.4 1.0 %copy-start.3 = (f32[128,4,2,128]{3,2,1,0:T(2,128)S(1)}, f32[128,4,2,128]{3,2,1,0:T(2,128)}, u32[]{:S(2)}) copy-start(f32[128,4,2,128]{3,2,1,0:T(2,128)} %param.12) | copy-start | bytes 1572868
  21.5 1.6 %copy-start.4 = (bf16[128,64,128]{2,1,0:T(8,128)(2,1)S(1)}, bf16[128,64,128]{2,1,0:T(8,128)(2,1)}, u32[]{:S(2)}) copy-start(bf16[128,64,128]{2,1,0:T(8,128)(2,1)} %features_ref.1) | copy-start | bytes 6291460
  23.1 0.9 %copy-start.5 = (bf16[1,256,256]{2,1,0:T(8,128)(2,1)S(1)}, bf16[1,256,256]{2,1,0:T(8,128)(2,1)}, u32[]{:S(2)}) copy-start(bf16[1,256,256]{2,1,0:T(8,128)(2,1)} %param.16) | copy-start | bytes 393220
  24.0 0.8 copy-start.6

commit v2 on v1

--- a/solution.py
+++ b/solution.py
@@ -9,7 +9,7 @@
 from jax.sharding import PartitionSpec as P
 
 kappa_most = 0.2
-GROUP = 4
+GROUP = 8
 CHUNK = 16
 F32 = jnp.float32
 BF16 = jnp.bfloat16
@@ -90,6 +90,7 @@
     cot_rows_ref,
     sea_rows_ref,
     lists,
+    list_mine,
     edge_out,
     edge_in,
     rows_out,
@@ -106,21 +107,22 @@
     lat_index = lax.axis_index("lat")
     peers = [("lon", d) for d in range(1, lon_count)] + [("lat", 1), ("lat", -1)]
     greet(peers)
+    list_mine[...] = jnp.broadcast_to(list_ref[...], list_mine.shape)
     copies = []
     for d in range(1, lon_count):
-        copies.append(push(list_ref, lists.at[d], (list_send, list_recv), d, "lon", d))
+        copies.append(push(list_mine, lists.at[d], (list_send, list_recv), d, "lon", d))
     for side, row in ((0, 0), (1, rows - 1)):
         rows_out[side, 0:subs] = state_ref[row]
         rows_out[side, subs : 2 * subs] = cot_ref[row]
         rows_out[side, 2 * subs : 2 * subs + 8] = jnp.broadcast_to(
-            sea_ref[row : row + 1], (8, width)
+            sea_ref[row : row + 1].astype(F32), (8, width)
         )
     halo = (halo_send, halo_recv)
     copies.append(push(rows_out.at[0], rows_in.at[1], halo, 0, "lat", -1))
     copies.append(push(rows_out.at[1], rows_in.at[0], halo, 1, "lat", 1))
     edge_out[:, 0:span] = pack_edges(state_ref[...].reshape(span, width))
     edge_out[:, span : 2 * span] = pack_edges(cot_ref[...].reshape(span, width))
-    edge_out[:, 2 * span :] = pack_edges(sea_ref[...])
+    edge_out[:, 2 * span :] = pack_edges(sea_ref[...].astype(F32))
     copies.append(push(edge_out, edge_in.at[1], halo, 2, "lon", -1))
     copies.append(push(edge_out, edge_in.at[0], halo, 3, "lon", 1))
     for copy in copies:
@@ -128,9 +130,9 @@
 
     me = lax.axis_index("lon")
     home = home_ref[...]
-    found = jnp.zeros(list_ref.shape, jnp.int32)
+    found = jnp.zeros(list_mine.shape, jnp.int32)
     for d in range(lon_count):
-        entries = list_ref[...] if d == 0 else lists[d]
+        entries = list_mine[...] if d == 0 else lists[d]
         owner = ring("lon", -d)
         source = entries // cap
         wanted = owner * cap + (entries - source * cap)
@@ -185,7 +187,7 @@
 
 def prepare_sea(sea_ref, sea_edge_ref, sea_rows_ref, open_refs):
     rows, width = sea_ref.shape
-    sea = sea_ref[...]
+    sea = sea_ref[...].astype(F32)
     edge = spread_edges(sea_edge_ref[...], width)
     south = jnp.concatenate([sea_rows_ref[0:1], sea[:-1]], axis=0)
     north = jnp.concatenate([sea[1:], sea_rows_ref[1:2]], axis=0)
@@ -207,7 +209,8 @@
     sea_rows_ref,
     w_in_ref,
     w_mid_ref,
-    small_ref,
+    bias_in_ref,
+    w_out_ref,
     bias_out_ref,
     diff_ref,
     diff_edge_ref,
@@ -224,6 +227,7 @@
     bias_in_col,
     w_out_rep,
     w_out_col,
+    bias_out_rep,
     acc_in,
     acc_mid,
     acc_out,
@@ -276,10 +280,20 @@
     lax.fori_loop(0, rows // CHUNK, kappa_chunk, 0)
     kgrad[pl.ds(rows, 8)] = jnp.zeros((8, subs, width), F32)
 
-    small_t = small_ref[...].T
-    bias_in_col[...] = jnp.broadcast_to(small_t[:, 8:9], (hid, width))
-    w_out_rep[...] = small_ref[0:8].astype(BF16)
-    w_out_col[...] = jnp.where(lane_of((hid, 8)) < 2, small_t[:, 0:8], 0.0).astype(BF16)
+    levels = w_out_ref.shape[1]
+    bias_in_col[...] = jnp.broadcast_to(bias_in_ref[...], (width, hid)).T
+    w_out = w_out_ref[...]
+    sub = lax.broadcasted_iota(jnp.int32, (8, levels), 0)
+    lev = lax.broadcasted_iota(jnp.int32, (8, levels), 1)
+    repeat = (lax.rem(sub, levels) == lev).astype(F32).astype(BF16)
+    single = (sub == lev).astype(F32).astype(BF16)
+    w_out_rep[...] = lax.dot_general(repeat, w_out, NT, preferred_element_type=F32).astype(BF16)
+    w_out_col[...] = lax.dot_general(w_out, single, NT, preferred_element_type=F32).astype(BF16)
+    level = lax.rem(lax.broadcasted_iota(jnp.int32, (8, width), 0), levels)
+    bias_out = jnp.zeros((8, width), F32)
+    for index in range(levels):
+        bias_out = jnp.where(level == index, bias_out_ref[index], bias_out)
+    bias_out_rep[...] = bias_out
     w_in_t[...] = w_in_ref[...].astype(F32).T.astype(BF16)
     w_mid_t[...] = w_mid_ref[...].astype(F32).T.astype(BF16)
     for ref in (acc_in, acc_mid, acc_out, acc_bias, acc_bout):
@@ -295,7 +309,7 @@
         h0 = jnp.tanh(first).astype(BF16)
         h1 = jnp.tanh(jnp.dot(w_mid_t[...], h0, preferred_element_type=F32)).astype(BF16)
         logits = jnp.dot(w_out_rep[...], h1, preferred_element_type=F32)
-        logits = logits + jnp.concatenate([bias_out_ref[...]] * GROUP, axis=1)
+        logits = logits + jnp.concatenate([bias_out_rep[...]] * GROUP, axis=1)
         squashed = 1.0 / (1.0 + jnp.exp(-logits))
         for i, row in enumerate(picked):
             diff_ref[row] = kappa_most * squashed[:, i * width : (i + 1) * width]
@@ -454,7 +468,8 @@
         return carry
 
     steps = rows // CHUNK
-    lax.fori_loop(0, steps // 2, chunk, 0)
+    quarter = steps // 4
+    lax.fori_loop(0, quarter, chunk, 0)
     for copy in reduce_lat:
         copy.wait()
     total = sums_ref[lat_me]
@@ -464,7 +479,7 @@
     reduce_lon = [
         push(for_lon.at[ring("lon", d)], from_lon.at[d], lon_sems, d, "lon", d) for d in lon_steps
     ]
-    lax.fori_loop(steps // 2, steps, chunk, 0)
+    lax.fori_loop(quarter, 2 * quarter, chunk, 0)
     for copy in reduce_lon:
         copy.wait()
     total = for_lon[lon_me]
@@ -475,12 +490,14 @@
     spread_lon = [
         push(chunk_sum, gathered.at[lon_me], lon_sems, lon_count + d, "lon", d) for d in lon_steps
     ]
+    lax.fori_loop(2 * quarter, 3 * quarter, chunk, 0)
     for copy in spread_lon:
         copy.wait()
     spread_lat = [
         push(gathered, full.at[lat_me], lat_sems, lat_count + d, "lat", d) for d in lat_steps
     ]
     full[lat_me] = gathered[...]
+    lax.fori_loop(3 * quarter, steps, chunk, 0)
     for copy in spread_lat:
         copy.wait()
 
@@ -523,7 +540,7 @@
 
     state = ocean_state.reshape(rows, subs, width)
     cot = cotangent.reshape(rows, subs, width)
-    sea = land_mask.astype(F32)
+    sea = land_mask
     span = rows * subs
     vmem = pl.BlockSpec(memory_space=pltpu.VMEM)
     smem = pl.BlockSpec(memory_space=pltpu.SMEM)
@@ -545,6 +562,7 @@
         out_specs=(vmem,) * 7,
         scratch_shapes=[
             pltpu.VMEM((lon_count, listed, rows), jnp.int32),
+            pltpu.VMEM((listed, rows), jnp.int32),
             pltpu.VMEM((8, 2 * span + rows), F32),
             pltpu.VMEM((2, 8, 2 * span + rows), F32),
             pltpu.VMEM((2, 2 * subs + 8, width), F32),
@@ -562,19 +580,9 @@
         cot,
         sea,
         home_slot.reshape(1, rows),
-        jnp.broadcast_to(owner_list, (listed, rows)),
+        owner_list,
     )
     flags = flags.reshape(rows)
-
-    small = jnp.concatenate(
-        [
-            jnp.tile(w_out.astype(F32).T, (8 // levels, 1)),
-            bias_in[None],
-            jnp.zeros((7, hid), F32),
-        ],
-        axis=0,
-    )
-    bias_out_rep = jnp.broadcast_to(jnp.tile(bias_out, (8 // levels,))[:, None], (8, width))
 
     tiles = (hid // width) * (hid + f_in + 8) // 8
     share = -(-tiles // (lat_count * lon_count))
@@ -588,7 +596,7 @@
             jax.ShapeDtypeStruct((8, span), F32),
             jax.ShapeDtypeStruct((lat_count * lon_count * share, 8, width), F32),
         ),
-        in_specs=[smem] + [vmem] * 14,
+        in_specs=[smem] + [vmem] * 14 + [smem],
         out_specs=(vmem,) * 3,
         scratch_shapes=[
             mask,
@@ -603,6 +611,7 @@
             pltpu.VMEM((hid, width), F32),
             pltpu.VMEM((8, hid), BF16),
             pltpu.VMEM((hid, 8), BF16),
+            pltpu.VMEM((8, width), F32),
             pltpu.VMEM((f_in, hid), F32),
             pltpu.VMEM((hid, hid), F32),
             pltpu.VMEM((8, hid), F32),
@@ -625,8 +634,9 @@
         sea_rows,
         w_in,
         w_mid[0],
-        small,
-        bias_out_rep,
+        bias_in[None],
+        w_out,
+        bias_out,
     )
 
     piece = (share, 8, width)

time: 77 us -> 69.6 us (0.904); the launches traced: 77.4 us -> 68.7 us
  Pallas kernels: 60.1 us -> 50.7 us
  local copies, waits for them, and re-layouts: 14.3 us -> 17.3 us
  other arithmetic: 2.28 us -> 0 us
    pallas_call x1, Pallas kernels: 43.3 us -> 22.9 us  [on_device(): pl.pallas_call(stencil_kernel, name='stencil', out_shape=(jax.ShapeDtypeS...]
    pallas_call x1, Pallas kernels: 4.66 us -> 15.6 us  [on_device(): pl.pallas_call(closure_kernel, name='closure', out_shape=(jax.ShapeDtypeS...]
    unnamed x23 -> x33, local copies, waits for them, and re-layouts: 12.7 us -> 17.3 us
    broadcast_in_dim x4 -> x0, local copies, waits for them, and re-layouts: 0.88 us -> none  [the longest x1 0.72 us: on_device(): jnp.broadcast_to(owner_list, (listed, rows))]
    convert_element_type x1 -> x0, other arithmetic: 0.85 us -> none  [on_device(): sea = land_mask.astype(F32)]
where the time goes in v2:
time: 69.6 us; the launch traced here: 68.7 us
  Pallas kernels  50.7 us (73%)
  local copies, waits for them, and re-layouts  17.3 us (25%)
    pallas_call x1, Pallas kernels, on_device(): pl.pallas_call(stencil_kernel, name='stencil', out_shape=(jax.ShapeDtypeS...  22.9 us
    unnamed x33, local copies, waits for them, and re-layouts  17.3 us
    pallas_call x1, Pallas kernels, on_device(): pl.pallas_call(closure_kernel, name='closure', out_shape=(jax.ShapeDtypeS...  15.6 us
    pallas_call x1, Pallas kernels, on_device(): pl.pallas_call(halo_kernel, name='halo', out_shape=(jax.ShapeDtypeStruct(...  12.2 us

profile of v2, /device:TPU:1, one launch (start us, length us, event | category | flops | bytes accessed | tf_op | source)
XLA Modules:
  0.0 68.7 jit_solution(1070676752421930050)
XLA Ops:
  0.6 0.7 %copy.18.list_ref = s32[32,1]{1,0:T(8,128)S(1)} copy(s32[32,1]{0,1:T(1,128)} %param.21) | data formatting | bytes 256 | tf_op args[10]
  1.4 0.8 %copy.19.w_out_ref = bf16[256,2]{1,0:T(8,128)(2,1)S(1)} copy(bf16[256,2]{0,1:T(2,128)(2,1)} %param.17) | data formatting | bytes 2048 | tf_op args[6]
  2.2 0.0 copy-start
  2.2 1.0 %copy-done = f32[128,4,2,128]{3,2,1,0:T(2,128)S(1)} copy-done((f32[128,4,2,128]{3,2,1,0:T(2,128)S(1)}, f32[128,4,2,128]{3,2,1,0:T(2,128)}, u32[]{:S(2)}) %copy-start) | copy-done | bytes 524312
  3.2 0.0 copy-start.2
  3.2 1.0 %copy-done.2 = f32[128,4,2,128]{3,2,1,0:T(2,128)S(1)} copy-done((f32[128,4,2,128]{3,2,1,0:T(2,128)S(1)}, f32[128,4,2,128]{3,2,1,0:T(2,128)}, u32[]{:S(2)}) %copy-start.2) | copy-done | bytes 524312
  4.3 0.0 copy-start.5
  4.3 0.8 %copy-done.5 = s32[128,128]{1,0:T(8,128)S(1)} copy-done((s32[128,128]{1,0:T(8,128)S(1)}, s32[128,128]{1,0:T(8,128)}, u32[]{:S(2)}) %copy-start.5) | copy-done | bytes 65560
  5.1 0.0 copy-start.10
  5.1 0.7 copy-done.10
  5.8 12.2 %halo.1 = (s32[1,128]{1,0:T(1,128)S(1)}, f32[8,1024]{1,0:T(8,128)S(1)}, f32[8,1024]{1,0:T(8,128)S(1)}, f32[8,128]{1,0:T(8,128)S(1)}, f32[2,8,128]{2,1,0:T(8,128)...) custom-call(f32[128,8,128]{2,1,0:T(8,128)S(1)} %bitcast.12, f32[128,8,128]{2,1,0:T(8,128)S(1)} %bitcast.15, ...), custom_call_target="tpu_custom_call" | custom-call | tf_op jit(solution)/shard_map/halo/pallas_call | solution.py:549
  17.9 0.0 copy-start.1
  17.9 1.0 %copy-done.1 = f32[128,4,2,128]{3,2,1,0:T(2,128)S(1)} copy-done((f32[128,4,2,128]{3,2,1,0:T(2,128)S(1)}, f32[128,4,2,128]{3,2,1,0:T(2,128)}, u32[]{:S(2)}) %copy-start.1) | copy-done | bytes 524312
  19.0 0.0 copy-start.3
  19.0 1.0 %copy-done.3 = f32[128,4,2,128]{3,2,1,0:T(2,128)S(1)} copy-done((f32[128,4,2,128]{3,2,1,0:T(2,128)S(1)}, f32[128,4,2,128]{3,2,1,0:T(2,128)}, u32[]{:S(2)}) %copy-start.3) | copy-done | bytes 524312
  20.0 0.0 copy-start.4
  20.0 1.6 %copy-done.4 = bf16[128,64,128]{2,1,0:T(8,128)(2,1)S(1)} copy-done((bf16[128,64,128]{2,1,0:T(8,128)(2,1)S(1)}, bf16[128,64,128]{2,1,0:T(8,128)(2,1)}, u32[]{:S(2)}) %copy-start.4) | copy-done | bytes 2097176
  21.6 0.0 copy-start.6
  21.6 0.8 %copy-done.6 = s32[128,128]{1,0:T(8,128)S(1)} copy-done((s32[128,128]{1,0:T(8,128)S(1)}, s32[128,128]{1,0:T(8,128)}, u32[]{:S(2)}) %copy-start.6) | copy-done | bytes 65560
  22.5 0.0 copy-start.7
  22.5 0.9 %copy-done.7 = bf16[1,256,256]{2,1,0:T(8,128)(2,1)S(1)} copy-done((bf16[1,256,256]{2,1,0:T(8,128)(2,1)S(1)}, bf16[1,256,256]{2,1,0:T(8,128)(2,1)}, u32[]{:S(2)}) %copy-start.7) | copy-done | bytes 131096
  23.4 0.0 copy-start.8
  23.4 0.8 %copy-done.8 = bf16[64,256]{1,0:T(8,128)(2,1)S(1)} copy-done((bf16[64,256]{1,0:T(8,128)(2,1)S(1)}, bf16[64,256]{1,0:T(8,128)(2,1)}, u32[]{:S(2)}) %copy-start.8) | copy-done | bytes 32792
  24.1 0.0 copy-start.9
  24.1 0.7 copy-done.9
  24.8 0.0 copy-start.11
  24.8 0.7 copy-done.11
  25.4 15.6 %closure.1 = (f32[136,8,128]{2,1,0:T(8,128)S(1)}, f32[8,1024]{1,0:T(8,128)S(1)}, f32[96,8,128]{2,1,0:T(8,128)S(1)}) custom-call(s32[128]{0:T(128)S(1)} %bitcast.26, bf16[128,64,128]{2,1,0:T(8,128)(2,1)S(1)} %copy-done.4, f32[128,8,128]{2,1,0:T(8,128)S(1)} %bitcast.13, f32[128,8,128]{2,1,0:T(8,128)S(1)} %bitcast.16, s32[128,128]{1,0:T(8,128)S(1)} %copy-done.6, ...), custom_call_target="tpu_custom_call" | custom-call | tf_op jit(solution)/shard_map/closure/pallas_call | solution.py:591
  41.1 22.9 %stencil.1 = (f32[128,8,128]{2,1,0:T(8,128)S(1)}, f32[128,8,128]{2,1,0:T(8,128)S(1)}, f32[64,256]{1,0:T(8,128)S(1)}, f32[1,256]{1,0:T(1,128)S(1)}, f32[256,256]{...) custom-call(f32[128,8,128]{2,1,0:T(8,128)S(1)} %bitcast.14, f32[128,8,128]{2,1,0:T(8,128)S(1)} %bitcast.17, ...), custom_call_target="tpu_custom_call" | custom-call | tf_op jit(solution)/shard_map/stencil/pallas_call | solution.py:643
  64.0 0.7 copy.20
  64.7 0.8 %copy.27 = f32[128,4,2,128]{3,2,1,0:T(2,128)} copy(f32[128,4,2,128]{3,2,1,0:T(2,128)S(1)} %bitcast.19) | data formatting | bytes 1048576
  65.5 0.8 %copy.28 = f32[128,4,2,128]{3,2,1,0:T(2,128)} copy(f32[128,4,2,128]{3,2,1,0:T(2,128)S(1)} %bitcast.18) | data formatting | bytes 1048576
  66.2 0.6 copy.29
  66.9 0.6 copy.30
  67.4 0.7 %copy.31 = f32[1,256,256]{2,1,0:T(8,128)} copy(f32[1,256,256]{2,1,0:T(8,128)S(1)} %bitcast.21) | data formatting | bytes 524288
  68.1 0.5 copy.32
Async XLA Ops:
  2.2 1.0 %copy-start = (f32[128,4,2,128]{3,2,1,0:T(2,128)S(1)}, f32[128,4,2,128]{3,2,1,0:T(2,128)}, u32[]{:S(2)}) copy-start(f32[128,4,2,128]{3,2,1,0:T(2,128)} %param.11) | copy-start | bytes 1572868
  3.2 1.0 %copy-start.2 = (f32[128,4,2,128]{3,2,1,0:T(2,128)S(1)}, f32[128,4,2,128]{3,2,1,0:T(2,128)}, u32[]{:S(2)}) copy-start(f32[128,4,2,128]{3,2,1,0:T(2,128)} %param.12) | copy-start | bytes 1572868
  4.3 0.8 %copy-start.5 = (s32[128,128]{1,0:T(8,128)S(1)}, s32[128,128]{1,0:T(8,128)}, u32[]{:S(2)}) copy-start(s32[128,128]{1,0:T(8,128)} %sea_ref.5) | copy-start | bytes 196612
  5.1 0.7 copy-start.10
  17.9 1.0 %copy-start.1 = (f32[128,4,2,128]{3,2,1,0:T(2,128)S(1)}, f32[128,4,2,128]{3,2,1,0:T(2,128)}, u32[]{:S(2)}) copy-start(f32[128,4,2,128]{3,2,1,0:T(2,128)} %param.11) | copy-start | bytes 1572868
  19.0 1.0 %copy-start.3 = (f32[128,4,2,128]{3,2,1,0:T(2,128)S(1)}, f32[128,4,2,128]{3,2,1,0:T(2,128)}, u32[]{:S(2)}) copy-start(f32[128,4,2,128]{3,2,1,0:T(2,128)} %param.12) | copy-start | bytes 1572868
  20.0 1.6 %copy-start.4 = (bf16[128,64,128]{2,1,0:T(8,128)(2,1)S(1)}, bf16[128,64,128]{2,1,0:T(8,128)(2,1)}, u32[]{:S(2)}) copy-start(bf16[128,64,128]{2,1,0:T(8,128)(2,1)} %features_ref.1) | copy-start | bytes 6291460
  21.6 0.8 %copy-start.6 = (s32[128,128]{1,0:T(8,128)S(1)}, s32[128,128]{1,0:T(8,128)}, u32[]{:S(2)}) copy-start(s32[128,128]{1,0:T(8,128)} %sea_ref.5) | copy-start | bytes 196612
  22.5 0.9 %copy-start.7 = (bf16[1,256,256]{2,1,0:T(8,128)(2,1)S(1)}, bf16[1,256,256]{2,1,0:T(8,128)(2,1)}, u32[]{:S(2)}) copy-start(bf16[1,256,256]{2,1,0:T(8,128)(2,1)} %param.16) | copy-start | bytes 393220
  23.4 0.8 %copy-start.8 = (bf16[64,256]{1,0:T(8,128)(2,1)S(1)}, bf16[64,256]{1,0:T(8,128)(2,1)}, u32[]{:S(2)}) copy-start(bf16[64,256]{1,0:T(8,128)(2,1)} %w_in_ref.1) | copy-start | bytes 98308
  24.1 0.7 copy-start.9
  24.8 0.7 copy-start.11
